TPU v7x, 256 devices: a whole 4x4x8 slice. The times are simulated.
256 devices in a mesh: head: 8 (over x, z_lo), ctx: 32 (over y, z_hi, core).
Axes of the slice: x: 4, y: 4, z: 8 (z_hi: 4, z_lo: 2; z = z_hi * 2 + z_lo), core: 2. Of those that a mesh axis runs over, the one named last changes fastest.
Arguments:
- queries: bfloat16 [16384, 5120], P(('head', 'ctx')), may hold values from -6 to 6
- keys: bfloat16 [16384, 5120], P(('head', 'ctx')), may hold values from -6 to 6
- values: bfloat16 [16384, 5120], P(('head', 'ctx')), may hold values from -6 to 6
- rates: bfloat16 [16384, 8], P(('head', 'ctx')), may hold values from 0.099609375 to 1
- q_gain: float32 [5120], replicated, may hold values from 0.1 to 1.9
- k_gain: float32 [5120], replicated, may hold values from 0.2 to 4.5, as said below
- w_first: float32 [8, 640, 640], P('head'), may hold values from -0.2766993 to 0.2766993
- w_second: float32 [8, 640, 640], P('head'), may hold values from -0.25 to 0.25
- w_third: float32 [8, 640, 640], P('head'), may hold values from -0.2766993 to 0.2766993
Outputs:
- attended: bfloat16 [16384, 5120], P(('head', 'ctx'))
Inputs may be any that keep to these rules, and one draw needn't show every extreme that they name: `k_gain`: positive per-feature gains.
All inputs are finite; a program needn't handle non-finite values.
Results may differ from a plain program's by a relative error of at most 0.015.
Values may be sent and summed in bfloat16 or wider, within the bound.
A program may use at most 64 MiB of HBM per device.

v0:
```python
import functools

import jax
import jax.numpy as jnp
from jax import lax
from jax.experimental import pallas as pl
from jax.experimental.pallas import tpu as pltpu
from jax.sharding import PartitionSpec as P

MESH = pl.DeviceIdType.MESH
F32 = jnp.float32
BF16 = jnp.bfloat16

epsilon = 1e-06
frob_eps = 1e-07
coeff_a = 3.4445
coeff_b = -4.775
coeff_c = 2.0315
step_size = 1.0

NY, NZ = 4, 4
VMEM_LIMIT = 54 * 2**20
PIECE = 24

ORDER = (
    "g0", "g1", "g2", "y0", "y1", "g3", "y2", "y3", "g4", "z0", "y4", "g5", "y5", "z1", "zg0",
    "z2", "zg1", "z3", "yg0", "zg2", "yg1", "z4", "zg3", "yg2", "z5", "c0", "c1", "zg4", "yg3",
    "n0", "n0", "zg5", "n0", "c2", "n0", "yg4", "c3", "n0", "n0", "n1", "yg5", "n1", "n1", "n1",
    "n1", "n1", "c4", "c5",
)


def dot(a, b):
    return jnp.dot(a, b, preferred_element_type=F32)


def dot_t(a, b):
    return lax.dot_general(a, b, (((1,), (1,)), ((), ())), preferred_element_type=F32)


def kernel(
    nh,
    q_hbm, k_hbm, v_hbm, r_hbm, qg_hbm, kg_hbm, w1_hbm, w2_hbm, w3_hbm,
    out,
    q_ref, k_ref, v_ref, r_ref, qg_ref, kg_ref, rb,
    sent, got, wf, wb, t1, t3, hid, d1, d3, kt, ht, e_ref,
    own, cs, cr, ys, yr, zq, zs, zr, zg, x0, xs, xm, x1, u, fw, ob,
    in_sem, a_ss, a_rs, c_ss, c_rs, y_ss, y_rs, z_ss, z_rs,
    zg_ss, zg_rs, yg_ss, yg_rs, cg_ss, cg_rs, o_ss, o_rs,
):
    me_h = lax.axis_index("head")
    me_c = lax.axis_index("ctx")
    y = me_c // (2 * NZ)
    z = (me_c // 2) % NZ
    core = me_c % 2
    tok, width = sent.shape[2], sent.shape[3]
    half = width // 2
    block = half // NY

    def head_peer(s):
        return (me_h + s) % nh

    def ctx_of(yy, zz, cc):
        return (yy * NZ + zz) * 2 + cc

    def z_dev(zz):
        return (me_h, ctx_of(y, zz, core))

    def y_dev(yy):
        return (me_h, ctx_of(yy, z, core))

    core_dev = (me_h, ctx_of(y, z, 1 - core))

    def remote(src, dst, ss, rs, dev):
        return pltpu.make_async_remote_copy(
            src_ref=src, dst_ref=dst, send_sem=ss, recv_sem=rs, device_id=dev, device_id_type=MESH
        )

    barrier = pltpu.get_barrier_semaphore()

    def greet(dev):
        pl.semaphore_signal(barrier, inc=1, device_id=dev, device_id_type=MESH)

    for s in range(1, nh):
        greet((head_peer(s), me_c))
    for s in range(1, NY):
        greet(y_dev((y + s) % NY))
    for s in range(1, NZ):
        greet(z_dev((z + s) % NZ))
    greet(core_dev)

    loads = [
        pltpu.make_async_copy(src, dst, in_sem.at[i])
        for i, (src, dst) in enumerate(
            [
                (k_hbm, k_ref), (kg_hbm, kg_ref), (v_hbm, v_ref), (r_hbm, r_ref),
                (q_hbm, q_ref), (qg_hbm, qg_ref),
                (w1_hbm.at[0], wf.at[0]), (w3_hbm.at[0], wf.at[2]), (w2_hbm.at[0], wf.at[1]),
            ]
        )
    ]
    for copy in loads:
        copy.start()

    def cols(j):
        return pl.ds(pl.multiple_of(j * width, 128), width)

    def send(t, fn):
        def step(s, carry):
            j = head_peer(s)
            sent[t, j] = fn(j)
            remote(
                sent.at[t, j], got.at[t, me_h], a_ss.at[t, j], a_rs.at[t, me_h], (j, me_c)
            ).start()
            return carry

        lax.fori_loop(1, nh, step, 0)
        got[t, me_h] = fn(me_h)

    def factor_of(x_ref):
        total = jnp.zeros((tok, 1), F32)
        for j in range(nh):
            x = x_ref[:, j * width : (j + 1) * width].astype(F32)
            total = total + jnp.sum(x * x, axis=-1, keepdims=True)
        return lax.rsqrt(total / (nh * width) + epsilon)

    def normalized(x_ref, g_ref, factor):
        return lambda j: (x_ref[:, cols(j)].astype(F32) * factor * g_ref[:, cols(j)]).astype(BF16)

    def arrived(t):
        def step(s, carry):
            j = head_peer(s)
            remote(
                sent.at[t, j], got.at[t, j], a_ss.at[t, j], a_rs.at[t, j], (j, me_c)
            ).wait()
            return carry

        lax.fori_loop(1, nh, step, 0)

    def rated(j):
        wide = jnp.concatenate([rb[j]] * (width // 128), axis=-1)
        return (wide * v_ref[:, cols(j)].astype(F32)).astype(BF16)

    loads[0].wait()
    loads[1].wait()
    factor = factor_of(k_ref)
    pl.semaphore_wait(barrier, nh - 1 + NY - 1 + NZ - 1 + 1)
    send(0, normalized(k_ref, kg_ref, factor))
    loads[2].wait()
    loads[3].wait()
    rate = r_ref[...].astype(F32).T
    for j in range(nh):
        rb[j] = jnp.broadcast_to(rate[:, j : j + 1], (tok, 128))
    send(1, rated)
    loads[4].wait()
    loads[5].wait()
    send(2, normalized(q_ref, qg_ref, factor_of(q_ref)))
    for i in range(3):
        loads[6 + i].wait()
    for i in range(3):
        wb[i] = wf[i].astype(BF16)

    tokens = nh * tok

    def whole(t):
        return got[t].reshape(tokens, width)

    arrived(0)
    p1 = dot(whole(0), wb[0])
    p3 = dot(whole(0), wb[2])
    sig = jax.nn.sigmoid(p1)
    act = p1 * sig
    hid[...] = (act * p3).astype(BF16)
    t3[...] = act
    t1[...] = p3 * sig * (1.0 + p1 * (1.0 - sig))
    kt[...] = whole(0).T
    ht[...] = hid[...].T
    arrived(1)
    e_ref[...] = whole(1)
    back = dot_t(whole(1), wb[1])
    d3[...] = (back * t3[...]).astype(BF16)
    d1[...] = (back * t1[...]).astype(BF16)

    cut = 3 * 128
    chunks = [(m, c) for m in range(3) for c in (slice(0, cut), slice(cut, width))]

    def half_rows(cc):
        return pl.ds(pl.multiple_of(cc * half, half), half)

    def core_copy(q):
        m, c = chunks[q]
        return remote(cs.at[m, :, c], cr.at[m, :, c], c_ss.at[q], c_rs.at[q], core_dev)

    def gradient(q, left, right):
        m, c = chunks[q]
        cs[m, :, c] = dot(left[half_rows(1 - core)], right[:, c]).astype(BF16)
        core_copy(q).start()
        own[m, :, c] = dot(left[half_rows(core)], right[:, c])

    def y_rows(j):
        return pl.ds(pl.multiple_of(j * block, 8), block)

    def z_rows(j):
        return pl.ds(pl.multiple_of(j * 16 + (j // 2) * 8, 8), PIECE)

    def y_copy(q, j, src):
        m, c = chunks[q]
        return remote(
            ys.at[m, j, :, c], yr.at[m, src, :, c], y_ss.at[q, j], y_rs.at[q, src], y_dev(j)
        )

    def z_copy(q, j, src):
        m, c = chunks[q]
        return remote(
            zs.at[m, j, :, c], zr.at[m, src, :, c], z_ss.at[q, j], z_rs.at[q, src], z_dev(j)
        )

    def zg_copy(q, j, src):
        m, c = chunks[q]
        slot = zg.at[m, src, :, c]
        return remote(slot, slot, zg_ss.at[q, j], zg_rs.at[q, src], z_dev(j))

    def yg_copy(q, j, src):
        m, c = chunks[q]
        slot = x0.at[m, core, src, :, c]
        return remote(slot, slot, yg_ss.at[q, j], yg_rs.at[q, src], y_dev(j))

    def cg_copy(q, cc, j):
        m, c = chunks[q]
        slot = x0.at[m, cc, j, :, c]
        return remote(slot, slot, cg_ss.at[q, j], cg_rs.at[q, j], core_dev)

    def start_y(q):
        m, c = chunks[q]
        core_copy(q).wait()
        own[m, :, c] = own[m, :, c] + cr[m, :, c].astype(F32)
        for s in (2, 1, 3):
            j = (y + s) % NY
            ys[m, j, :, c] = own[m, y_rows(j), c].astype(BF16)
            y_copy(q, j, y).start()

    def start_z(q):
        m, c = chunks[q]
        total = own[m, y_rows(y), c]
        for s in range(1, NY):
            j = (y + s) % NY
            y_copy(q, j, y).wait_send()
            y_copy(q, j, j).wait_recv()
            total = total + yr[m, j, :, c].astype(F32)
        zq[m, :, c] = total
        for s in range(1, NZ):
            j = (z + s) % NZ
            zs[m, j, :, c] = zq[m, z_rows(j), c].astype(BF16)
            z_copy(q, j, z).start()

    def start_zg(q):
        m, c = chunks[q]
        total = zq[m, z_rows(z), c]
        for s in range(1, NZ):
            j = (z + s) % NZ
            z_copy(q, j, z).wait_send()
            z_copy(q, j, j).wait_recv()
            total = total + zr[m, j, :, c].astype(F32)
        zg[m, z, :, c] = total.astype(BF16)
        for s in range(1, NZ):
            zg_copy(q, (z + s) % NZ, z).start()

    def start_yg(q):
        m, c = chunks[q]
        for s in range(1, NZ):
            j = (z + s) % NZ
            zg_copy(q, j, z).wait_send()
            zg_copy(q, j, j).wait_recv()
        parts = [zg[m, j, :, c].astype(F32) for j in range(NZ)]
        total = jnp.concatenate([parts[0][:16], parts[1], parts[2][:16], parts[3]], axis=0)
        x0[m, core, y, :, c] = total.astype(BF16)
        for s in (2, 1, 3):
            yg_copy(q, (y + s) % NY, y).start()
        cg_copy(q, core, y).start()

    def start_cg(q):
        for s in (1, 3, 2):
            j = (y + s) % NY
            yg_copy(q, j, y).wait_send()
            yg_copy(q, j, j).wait_recv()
            cg_copy(q, core, j).start()

    def gathered(m):
        for q in (2 * m, 2 * m + 1):
            for j in range(NY):
                cg_copy(q, core, j).wait_send()
                cg_copy(q, 1 - core, j).wait_recv()

    def ns_steps(m, w_index):
        cell = {}

        def grad():
            return x0[m].reshape(width, width)

        def square0():
            gathered(m)
            g = grad().astype(F32)
            inv = 1.0 / (jnp.sqrt(jnp.sum(g * g, axis=(0, 1), keepdims=True)) + frob_eps)
            cell["inv"] = inv
            xs[...] = (dot_t(grad(), grad()) * inv * inv).astype(BF16)

        def poly():
            s = xs[...]
            xm[...] = (coeff_b * s.astype(F32) + coeff_c * dot(s, s)).astype(BF16)

        def step0():
            g = grad()
            x1[...] = ((coeff_a * g.astype(F32) + dot(xm[...], g)) * cell["inv"]).astype(BF16)

        def square1():
            xs[...] = dot_t(x1[...], x1[...]).astype(BF16)

        def step1():
            new = (coeff_a * x1[...].astype(F32) + dot(xm[...], x1[...])).astype(BF16)
            u[m] = (wf[w_index] + step_size * new.astype(F32)).astype(BF16)

        return [square0, poly, step0, square1, poly, step1]

    factors = ((kt, d3), (kt, d1), (ht, e_ref))
    iterations = [iter(ns_steps(0, 2)), iter(ns_steps(1, 0))]

    def start_g(q):
        gradient(q, *factors[q // 2])

    stages = {
        "g": start_g, "y": start_y, "z": start_z, "zg": start_zg, "yg": start_yg, "c": start_cg,
    }
    for event in ORDER:
        name, index = event[:-1], int(event[-1])
        if name == "n":
            next(iterations[index])()
        else:
            stages[name](index)

    arrived(2)
    a = dot(whole(2), u[1])
    b = dot(whole(2), u[0])
    fw[...] = (a * jax.nn.sigmoid(a) * b).astype(BF16)
    for fn in ns_steps(2, 1):
        fn()

    def o_copy(j, src):
        return remote(ob.at[j], out.at[src], o_ss.at[j], o_rs.at[src], (j, me_c))

    chunk = 2 * tok
    n_chunks = tokens // chunk
    mine = me_h // 2

    def finish(i):
        c = (mine + i) % n_chunks
        rows = pl.ds(pl.multiple_of(c * chunk, chunk), chunk)
        o = dot(fw[rows], u[2])
        o = o * lax.rsqrt(jnp.mean(o * o, axis=-1, keepdims=True) + epsilon)
        ob[pl.ds(2 * c, 2)] = o.astype(BF16).reshape(2, tok, width)
        return c

    def others(i, carry):
        c = finish(i)
        o_copy(2 * c, me_h).start()
        o_copy(2 * c + 1, me_h).start()
        return carry

    lax.fori_loop(1, n_chunks, others, 0)
    finish(0)
    o_copy(mine * 2 + (1 - me_h % 2), me_h).start()
    keep = pltpu.make_async_copy(ob.at[me_h], out.at[me_h], in_sem.at[0])
    keep.start()

    def returned(s, carry):
        j = head_peer(s)
        o_copy(j, me_h).wait_send()
        o_copy(j, j).wait_recv()
        return carry

    lax.fori_loop(1, nh, returned, 0)
    keep.wait()


def per_device(queries, keys, values, rates, q_gain, k_gain, w_first, w_second, w_third):
    nh = rates.shape[1]
    tok, model = queries.shape
    width = model // nh
    tokens = nh * tok
    half = width // 2
    block = half // NY
    hbm = pl.BlockSpec(memory_space=pl.ANY)

    def dma(*shape):
        return pltpu.SemaphoreType.DMA(shape)

    out = pl.pallas_call(
        functools.partial(kernel, nh),
        out_shape=jax.ShapeDtypeStruct((nh, tok, width), BF16),
        in_specs=[hbm] * 9,
        out_specs=hbm,
        scratch_shapes=[
            pltpu.VMEM((tok, model), BF16),
            pltpu.VMEM((tok, model), BF16),
            pltpu.VMEM((tok, model), BF16),
            pltpu.VMEM((nh, tok), BF16),
            pltpu.VMEM((1, model), F32),
            pltpu.VMEM((1, model), F32),
            pltpu.VMEM((nh, tok, 128), F32),
            pltpu.VMEM((3, nh, tok, width), BF16),
            pltpu.VMEM((3, nh, tok, width), BF16),
            pltpu.VMEM((3, width, width), F32),
            pltpu.VMEM((3, width, width), BF16),
            pltpu.VMEM((tokens, width), F32),
            pltpu.VMEM((tokens, width), F32),
            pltpu.VMEM((tokens, width), BF16),
            pltpu.VMEM((tokens, width), BF16),
            pltpu.VMEM((tokens, width), BF16),
            pltpu.VMEM((width, tokens), BF16),
            pltpu.VMEM((width, tokens), BF16),
            pltpu.VMEM((tokens, width), BF16),
            pltpu.VMEM((3, half, width), F32),
            pltpu.VMEM((3, half, width), BF16),
            pltpu.VMEM((3, half, width), BF16),
            *[pltpu.VMEM((3, NY, block, width), BF16)] * 2,
            pltpu.VMEM((3, block, width), F32),
            pltpu.VMEM((3, NZ, PIECE, width), BF16),
            pltpu.VMEM((3, NZ, PIECE, width), BF16),
            pltpu.VMEM((3, NZ, PIECE, width), BF16),
            pltpu.VMEM((3, 2, NY, block, width), BF16),
            pltpu.VMEM((width, width), BF16),
            pltpu.VMEM((width, width), BF16),
            pltpu.VMEM((width, width), BF16),
            pltpu.VMEM((3, width, width), BF16),
            pltpu.VMEM((tokens, width), BF16),
            pltpu.VMEM((nh, tok, width), BF16),
            dma(9),
            dma(3, nh), dma(3, nh),
            dma(6), dma(6),
            *[dma(6, NY)] * 2,
            *[dma(6, NZ)] * 4,
            *[dma(6, NY)] * 4,
            dma(nh), dma(nh),
        ],
        compiler_params=pltpu.CompilerParams(
            collective_id=0, has_side_effects=True, vmem_limit_bytes=VMEM_LIMIT
        ),
        name="span",
    )(
        queries, keys, values, rates.T, q_gain.reshape(1, model), k_gain.reshape(1, model),
        w_first, w_second, w_third,
    )
    return out.transpose(1, 0, 2).reshape(tok, model)


def solution(mesh):
    return jax.shard_map(
        per_device,
        mesh=mesh,
        in_specs=(
            P(("head", "ctx"), None),
            P(("head", "ctx"), None),
            P(("head", "ctx"), None),
            P(("head", "ctx"), None),
            P(),
            P(),
            P("head", None, None),
            P("head", None, None),
            P("head", None, None),
        ),
        out_specs=P(("head", "ctx"), None),
        check_vma=False,
    )
```

profile of v0, /device:TPU:1, one launch (start us, length us, event | category | flops | bytes accessed | tf_op | source)
XLA Modules:
  0.0 89.7 jit_solution(4210710952577688921)
XLA Ops:
  0.0 87.7 %span.1 = bf16[8,64,640]{2,1,0:T(8,128)(2,1)} custom-call(bf16[64,5120]{1,0:T(8,128)(2,1)} %q_hbm.1, bf16[64,5120]{1,0:T(8,128)(2,1)} %k_hbm.1, bf16[64,5120]{1,0:T(8,128)(2,1)} %v_hbm.1, bf16[8,64]{1,0:T(8,128)(2,1)} %bitcast.9, f32[1,5120]{1,0:T(1,128)} %bitcast.7, f32[1,5120]{1,0:T(1,128)} %bitcast.8, f32[1,640,640]{2,1,0:T(8,128)} %w1_hbm.1, ...), custom_call_target="tpu_custom_call" | custom-call | tf_op jit(solution)/shard_map/span/pallas_call | solution.py:396
  87.7 2.0 %copy.11 = bf16[8,8,8,640]{3,2,0,1:T(8,128)(2,1)} copy(bf16[8,8,8,640]{3,2,1,0:T(8,128)(2,1)} %bitcast.6) | data formatting | bytes 1310720 | tf_op jit(solution)/shard_map/reshape | solution.py:452
where the time goes:
time: 89.8 us; the launch traced here: 89.7 us
  Pallas kernels  87.7 us (98%)
  local copies, waits for them, and re-layouts  1.99 us (2%)
    pallas_call x1, Pallas kernels, per_device(): pl.pallas_call(functools.partial(kernel, nh), out_shape=jax.ShapeDtypeStr...  87.7 us
    reshape x1, local copies, waits for them, and re-layouts, per_device(): return out.transpose(1, 0, 2).reshape(tok, model)  1.99 us

commit v1 on v0

--- a/solution.py
+++ b/solution.py
@@ -20,13 +20,14 @@
 
 NY, NZ = 4, 4
 VMEM_LIMIT = 54 * 2**20
+CUTS = (0, 2, 5)
 PIECE = 24
 
 ORDER = (
-    "g0", "g1", "g2", "y0", "y1", "g3", "y2", "y3", "g4", "z0", "y4", "g5", "y5", "z1", "zg0",
-    "z2", "zg1", "z3", "yg0", "zg2", "yg1", "z4", "zg3", "yg2", "z5", "c0", "c1", "zg4", "yg3",
-    "n0", "n0", "zg5", "n0", "c2", "n0", "yg4", "c3", "n0", "n0", "n1", "yg5", "n1", "n1", "n1",
-    "n1", "n1", "c4", "c5",
+    "g0", "g1", "g2", "y0", "y1", "g3", "g4", "z0", "y3", "y2", "y4", "z1", "g5", "zg0", "z3",
+    "y5", "zg1", "z2", "z4", "yg0", "zg3", "z5", "yg1", "zg2", "zg4", "c0", "yg3", "zg5", "c1",
+    "yg2", "n0", "yg4", "n0", "n0", "n0", "c3", "yg5", "c2", "n0", "n0", "n1", "n1", "n1", "n1",
+    "n1", "n1", "c5", "c4",
 )
 
 
@@ -132,7 +133,7 @@
             j = head_peer(s)
             remote(
                 sent.at[t, j], got.at[t, j], a_ss.at[t, j], a_rs.at[t, j], (j, me_c)
-            ).wait()
+            ).wait_recv()
             return carry
 
         lax.fori_loop(1, nh, step, 0)
@@ -181,8 +182,8 @@
     d3[...] = (back * t3[...]).astype(BF16)
     d1[...] = (back * t1[...]).astype(BF16)
 
-    cut = 3 * 128
-    chunks = [(m, c) for m in range(3) for c in (slice(0, cut), slice(cut, width))]
+    chunks = [(m, slice(a * 128, b * 128)) for m in range(3) for a, b in zip(CUTS, CUTS[1:])]
+    per_matrix = len(CUTS) - 1
 
     def half_rows(cc):
         return pl.ds(pl.multiple_of(cc * half, half), half)
@@ -230,21 +231,23 @@
         slot = x0.at[m, cc, j, :, c]
         return remote(slot, slot, cg_ss.at[q, j], cg_rs.at[q, j], core_dev)
 
+    def pair_sum(q, j):
+        m, c = chunks[q]
+        return own[m, y_rows(j), c] + cr[m, pl.ds(pl.multiple_of(j * block, 16), block), c].astype(F32)
+
     def start_y(q):
         m, c = chunks[q]
-        core_copy(q).wait()
-        own[m, :, c] = own[m, :, c] + cr[m, :, c].astype(F32)
+        core_copy(q).wait_recv()
         for s in (2, 1, 3):
             j = (y + s) % NY
-            ys[m, j, :, c] = own[m, y_rows(j), c].astype(BF16)
+            ys[m, j, :, c] = pair_sum(q, j).astype(BF16)
             y_copy(q, j, y).start()
 
     def start_z(q):
         m, c = chunks[q]
-        total = own[m, y_rows(y), c]
+        total = pair_sum(q, y)
         for s in range(1, NY):
             j = (y + s) % NY
-            y_copy(q, j, y).wait_send()
             y_copy(q, j, j).wait_recv()
             total = total + yr[m, j, :, c].astype(F32)
         zq[m, :, c] = total
@@ -258,7 +261,6 @@
         total = zq[m, z_rows(z), c]
         for s in range(1, NZ):
             j = (z + s) % NZ
-            z_copy(q, j, z).wait_send()
             z_copy(q, j, j).wait_recv()
             total = total + zr[m, j, :, c].astype(F32)
         zg[m, z, :, c] = total.astype(BF16)
@@ -269,7 +271,6 @@
         m, c = chunks[q]
         for s in range(1, NZ):
             j = (z + s) % NZ
-            zg_copy(q, j, z).wait_send()
             zg_copy(q, j, j).wait_recv()
         parts = [zg[m, j, :, c].astype(F32) for j in range(NZ)]
         total = jnp.concatenate([parts[0][:16], parts[1], parts[2][:16], parts[3]], axis=0)
@@ -281,14 +282,12 @@
     def start_cg(q):
         for s in (1, 3, 2):
             j = (y + s) % NY
-            yg_copy(q, j, y).wait_send()
             yg_copy(q, j, j).wait_recv()
             cg_copy(q, core, j).start()
 
     def gathered(m):
-        for q in (2 * m, 2 * m + 1):
+        for q in range(per_matrix * m, per_matrix * (m + 1)):
             for j in range(NY):
-                cg_copy(q, core, j).wait_send()
                 cg_copy(q, 1 - core, j).wait_recv()
 
     def ns_steps(m, w_index):
@@ -325,7 +324,7 @@
     iterations = [iter(ns_steps(0, 2)), iter(ns_steps(1, 0))]
 
     def start_g(q):
-        gradient(q, *factors[q // 2])
+        gradient(q, *factors[q // per_matrix])
 
     stages = {
         "g": start_g, "y": start_y, "z": start_z, "zg": start_zg, "yg": start_yg, "c": start_cg,
@@ -371,8 +370,23 @@
     keep = pltpu.make_async_copy(ob.at[me_h], out.at[me_h], in_sem.at[0])
     keep.start()
 
+    for q in range(len(chunks)):
+        core_copy(q).wait_send()
+        for s in range(1, NY):
+            y_copy(q, (y + s) % NY, y).wait_send()
+            yg_copy(q, (y + s) % NY, y).wait_send()
+        for s in range(1, NZ):
+            z_copy(q, (z + s) % NZ, z).wait_send()
+            zg_copy(q, (z + s) % NZ, z).wait_send()
+        for j in range(NY):
+            cg_copy(q, core, j).wait_send()
+
     def returned(s, carry):
         j = head_peer(s)
+        for t in range(3):
+            remote(
+                sent.at[t, j], got.at[t, j], a_ss.at[t, j], a_rs.at[t, j], (j, me_c)
+            ).wait_send()
         o_copy(j, me_h).wait_send()
         o_copy(j, j).wait_recv()
         return carry

time: 89.8 us -> 87.1 us (0.970)
  Pallas kernels: 87.7 us -> 85 us
    pallas_call x1, Pallas kernels: 87.7 us -> 85 us  [per_device(): pl.pallas_call(functools.partial(kernel, nh), out_shape=jax.ShapeDtypeStr...]
where the time goes in v1:
time: 87.1 us; the launch traced here: 87 us
  Pallas kernels  85 us (98%)
  local copies, waits for them, and re-layouts  1.99 us (2%)
    pallas_call x1, Pallas kernels, per_device(): pl.pallas_call(functools.partial(kernel, nh), out_shape=jax.ShapeDtypeStr...  85 us
    reshape x1, local copies, waits for them, and re-layouts, per_device(): return out.transpose(1, 0, 2).reshape(tok, model)  1.99 us

profile of v1, /device:TPU:1, one launch (start us, length us, event | category | flops | bytes accessed | tf_op | source)
XLA Modules:
  0.0 87.0 jit_solution(14161768385149968749)
XLA Ops:
  0.0 85.0 %span.1 = bf16[8,64,640]{2,1,0:T(8,128)(2,1)} custom-call(bf16[64,5120]{1,0:T(8,128)(2,1)} %q_hbm.1, bf16[64,5120]{1,0:T(8,128)(2,1)} %k_hbm.1, bf16[64,5120]{1,0:T(8,128)(2,1)} %v_hbm.1, bf16[8,64]{1,0:T(8,128)(2,1)} %bitcast.9, f32[1,5120]{1,0:T(1,128)} %bitcast.7, f32[1,5120]{1,0:T(1,128)} %bitcast.8, f32[1,640,640]{2,1,0:T(8,128)} %w1_hbm.1, ...), custom_call_target="tpu_custom_call" | custom-call | tf_op jit(solution)/shard_map/span/pallas_call | solution.py:410
  85.0 2.0 %copy.11 = bf16[8,8,8,640]{3,2,0,1:T(8,128)(2,1)} copy(bf16[8,8,8,640]{3,2,1,0:T(8,128)(2,1)} %bitcast.6) | data formatting | bytes 1310720 | tf_op jit(solution)/shard_map/reshape | solution.py:466

commit v2 on v1

--- a/solution.py
+++ b/solution.py
@@ -108,7 +108,7 @@
 
     def send(t, fn):
         def step(s, carry):
-            j = head_peer(s)
+            j = head_peer((s + nh // 2 - 2) % (nh - 1) + 1)
             sent[t, j] = fn(j)
             remote(
                 sent.at[t, j], got.at[t, me_h], a_ss.at[t, j], a_rs.at[t, me_h], (j, me_c)
@@ -251,7 +251,7 @@
             y_copy(q, j, j).wait_recv()
             total = total + yr[m, j, :, c].astype(F32)
         zq[m, :, c] = total
-        for s in range(1, NZ):
+        for s in (2, 1, 3):
             j = (z + s) % NZ
             zs[m, j, :, c] = zq[m, z_rows(j), c].astype(BF16)
             z_copy(q, j, z).start()
@@ -264,7 +264,7 @@
             z_copy(q, j, j).wait_recv()
             total = total + zr[m, j, :, c].astype(F32)
         zg[m, z, :, c] = total.astype(BF16)
-        for s in range(1, NZ):
+        for s in (2, 1, 3):
             zg_copy(q, (z + s) % NZ, z).start()
 
     def start_yg(q):

time: 87.1 us -> 89.5 us (1.028)
  Pallas kernels: 85 us -> 87.4 us
    pallas_call x1, Pallas kernels: 85 us -> 87.4 us  [per_device(): pl.pallas_call(functools.partial(kernel, nh), out_shape=jax.ShapeDtypeStr...]
where the time goes in v2:
time: 89.5 us; the launch traced here: 89.4 us
  Pallas kernels  87.4 us (98%)
  local copies, waits for them, and re-layouts  1.99 us (2%)
    pallas_call x1, Pallas kernels, per_device(): pl.pallas_call(functools.partial(kernel, nh), out_shape=jax.ShapeDtypeStr...  87.4 us
    reshape x1, local copies, waits for them, and re-layouts, per_device(): return out.transpose(1, 0, 2).reshape(tok, model)  1.99 us

profile of v2, /device:TPU:1, one launch (start us, length us, event | category | flops | bytes accessed | tf_op | source)
XLA Modules:
  0.0 89.4 jit_solution(3580969216528372742)
XLA Ops:
  0.0 87.4 %span.1 = bf16[8,64,640]{2,1,0:T(8,128)(2,1)} custom-call(bf16[64,5120]{1,0:T(8,128)(2,1)} %q_hbm.1, bf16[64,5120]{1,0:T(8,128)(2,1)} %k_hbm.1, bf16[64,5120]{1,0:T(8,128)(2,1)} %v_hbm.1, bf16[8,64]{1,0:T(8,128)(2,1)} %bitcast.9, f32[1,5120]{1,0:T(1,128)} %bitcast.7, f32[1,5120]{1,0:T(1,128)} %bitcast.8, f32[1,640,640]{2,1,0:T(8,128)} %w1_hbm.1, ...), custom_call_target="tpu_custom_call" | custom-call | tf_op jit(solution)/shard_map/span/pallas_call | solution.py:410
  87.4 2.0 %copy.11 = bf16[8,8,8,640]{3,2,0,1:T(8,128)(2,1)} copy(bf16[8,8,8,640]{3,2,1,0:T(8,128)(2,1)} %bitcast.6) | data formatting | bytes 1310720 | tf_op jit(solution)/shard_map/reshape | solution.py:466
